TPU v7x, 32 devices: a whole 2x2x4 slice. The times are simulated.
32 devices in a mesh: section: 4 (over x, core), ctx: 8 (over z, y).
Axes of the slice: x: 2, y: 2, z: 4, core: 2. Of those that a mesh axis runs over, the one named last changes fastest.
Arguments:
- block_order: int32 [8], replicated, may hold values from 0 to 7, each once
- queries: bfloat16 [4, 64, 2560], P('section', 'ctx'), may hold values from -400 to 400
- cache_keys: bfloat16 [1024, 2560], P('ctx', 'section'), may hold values from -6 to 6
- cache_values: bfloat16 [1024, 2560], P('ctx', 'section'), may hold values from -6 to 6
- attention_out: bfloat16 [4, 64, 2560], P('section', 'ctx'), may hold values from -6 to 6
- output_grad: bfloat16 [4, 64, 2560], P('section', 'ctx'), may hold values from -192 to 192
Outputs:
- grad_queries: bfloat16 [4, 64, 2560], P('section', 'ctx')
- grad_keys: bfloat16 [1024, 2560], P('ctx', 'section')
- grad_values: bfloat16 [1024, 2560], P('ctx', 'section')
Inputs may be any that keep to these rules, and one draw needn't show every extreme that they name: `block_order`: every block number once.
All inputs are finite; a program needn't handle non-finite values.
Results may differ from a plain program's by a relative error of at most 0.012.
Values may be sent and summed in bfloat16 or wider, within the bound.
No kernel may reach another device: no remote copies, remote signals or barrier semaphores. Data moves between devices by JAX's collectives and lax.ppermute only.
A program may use at most 64 MiB of HBM per device.

v0:
```python
import jax
import jax.numpy as jnp
from jax import lax
from jax.sharding import PartitionSpec as P

HEADS = 20
HEAD_DIM = 128
masked_score = -1e30


def local(block_order, queries, cache_keys, cache_values, attention_out, output_grad):
    ctx_count = lax.axis_size("ctx")
    rows_here = queries.shape[1]
    key_count = cache_keys.shape[0]
    key_total = key_count * ctx_count
    query_count = rows_here * ctx_count
    scaling = HEAD_DIM ** (-0.5)
    product = output_grad.astype(jnp.float32) * attention_out.astype(jnp.float32)
    delta_terms = jnp.sum(product.reshape(1, rows_here, HEADS, HEAD_DIM), axis=3)
    query_part, grad_part, delta_part = (queries, output_grad, delta_terms)
    key_block, value_block = (
        lax.all_gather(cache_keys, "section", axis=1, tiled=True),
        lax.all_gather(cache_values, "section", axis=1, tiled=True),
    )
    group_heads = HEADS
    layers = query_part.shape[0]
    pair_count = layers * group_heads
    query_all, grad_all = (
        lax.all_gather(query_part, "ctx", axis=1, tiled=True),
        lax.all_gather(grad_part, "ctx", axis=1, tiled=True),
    )
    delta_all = lax.all_gather(delta_part, "ctx", axis=1, tiled=True)

    def split_heads(values):
        return (
            values.reshape(layers, query_count, group_heads, HEAD_DIM)
            .transpose(0, 2, 1, 3)
            .reshape(pair_count, query_count, HEAD_DIM)
        )

    query_heads = split_heads(query_all)
    grad_heads = split_heads(grad_all)
    delta_heads = delta_all.transpose(0, 2, 1).reshape(pair_count, query_count)
    key_heads = key_block.reshape(key_count, group_heads, HEAD_DIM).transpose(1, 0, 2)
    value_heads = value_block.reshape(key_count, group_heads, HEAD_DIM).transpose(1, 0, 2)
    head_ids = jnp.arange(pair_count, dtype=jnp.int32) % group_heads
    ctx_index = lax.axis_index("ctx")
    key_pos = block_order[ctx_index] * key_count + jnp.arange(key_count, dtype=jnp.int32)
    query_pos = key_total - query_count + jnp.arange(query_count, dtype=jnp.int32)
    visible = key_pos[None, :] <= query_pos[:, None]

    def masked_scores(query_head, head_index):
        scores = (
            jnp.dot(query_head, key_heads[head_index].T, preferred_element_type=jnp.float32)
            * scaling
        )
        return jnp.where(visible, scores, masked_score)

    def local_stats(packed):
        query_head, head_index = packed
        scores = masked_scores(query_head, head_index)
        row_max = jnp.max(scores, axis=1)
        row_sum = jnp.sum(jnp.where(visible, jnp.exp(scores - row_max[:, None]), 0.0), axis=1)
        return (row_max, row_sum)

    row_max, row_sum = lax.map(local_stats, (query_heads, head_ids))
    peak_max = lax.pmax(row_max.astype(jnp.bfloat16), "ctx").astype(row_max.dtype)
    row_sum = lax.psum(row_sum * jnp.exp(row_max - peak_max), "ctx")
    row_max = peak_max
    log_total = row_max + jnp.log(row_sum)

    def gradients(packed):
        query_head, grad_head, delta_head, total_head, head_index = packed
        scores = masked_scores(query_head, head_index)
        prob = jnp.where(visible, jnp.exp(scores - total_head[:, None]), 0.0)
        prob_b = prob.astype(jnp.bfloat16)
        value_grad = jnp.dot(prob_b.T, grad_head, preferred_element_type=jnp.float32)
        prob_grad = jnp.dot(
            grad_head, value_heads[head_index].T, preferred_element_type=jnp.float32
        )
        score_grad = (prob * (prob_grad - delta_head[:, None]) * scaling).astype(jnp.bfloat16)
        query_grad = jnp.dot(score_grad, key_heads[head_index], preferred_element_type=jnp.float32)
        key_grad = jnp.dot(score_grad.T, query_head, preferred_element_type=jnp.float32)
        return (query_grad, key_grad, value_grad)

    query_grad, key_grad, value_grad = lax.map(
        gradients, (query_heads, grad_heads, delta_heads, log_total, head_ids)
    )
    query_layout = (
        query_grad.reshape(layers, group_heads, query_count, HEAD_DIM)
        .transpose(0, 2, 1, 3)
        .reshape(layers, query_count, group_heads * HEAD_DIM)
    )
    query_rows_sum = lax.psum_scatter(query_layout, "ctx", scatter_dimension=1, tiled=True)
    key_sum = (
        key_grad.reshape(layers, group_heads, key_count, HEAD_DIM)
        .sum(axis=0)
        .transpose(1, 0, 2)
        .reshape(key_count, group_heads * HEAD_DIM)
    )
    value_sum = (
        value_grad.reshape(layers, group_heads, key_count, HEAD_DIM)
        .sum(axis=0)
        .transpose(1, 0, 2)
        .reshape(key_count, group_heads * HEAD_DIM)
    )
    grad_queries = query_rows_sum.astype(jnp.bfloat16)
    key_part, value_part = (
        lax.psum_scatter(
            key_sum.astype(jnp.bfloat16), "section", scatter_dimension=1, tiled=True
        ).astype(jnp.float32),
        lax.psum_scatter(
            value_sum.astype(jnp.bfloat16), "section", scatter_dimension=1, tiled=True
        ).astype(jnp.float32),
    )
    grad_keys = key_part.astype(jnp.bfloat16)
    grad_values = value_part.astype(jnp.bfloat16)
    return (grad_queries, grad_keys, grad_values)


def solution(mesh):
    in_specs = (
        P(),
        P("section", "ctx", None),
        P("ctx", "section"),
        P("ctx", "section"),
        P("section", "ctx", None),
        P("section", "ctx", None),
    )
    out_specs = (P("section", "ctx", None), P("ctx", "section"), P("ctx", "section"))
    return jax.shard_map(local, mesh=mesh, in_specs=in_specs, out_specs=out_specs, check_vma=False)
```

profile of v0, /device:TPU:0, one launch (start us, length us, event | category | flops | bytes accessed | tf_op | source)
XLA Modules:
  0.0 449.6 jit_solution(16274756989076429292)
XLA Ops:
  9.2 33.0 %all_gather.17 = bf16[1,64,2560]{2,1,0:T(8,128)(2,1)S(1)} all-gather(bf16[1,8,2560]{2,1,0:T(8,128)(2,1)} %param.15), channel_id=1, replica_groups=mesh['section'=4,'ctx'=8] {'ctx'}, dimensions={1}, use_global_device_ids=true | all-gather | bytes 368640 | tf_op jit(solution)/shard_map/all_gather | solution.py:30
  42.4 30.6 %all-gather = f32[64,20]{1,0:T(8,128)S(1)} all-gather(f32[8,20]{1,0:T(8,128)S(1)} %copy.43), channel_id=2, replica_groups=mesh['section'=4,'ctx'=8] {'ctx'}, dimensions={0}, use_global_device_ids=true | all-gather | bytes 5760 | tf_op jit(solution)/shard_map/all_gather | solution.py:32
  74.8 30.8 %all_gather.15 = bf16[1,64,2560]{2,1,0:T(8,128)(2,1)S(1)} all-gather(bf16[1,8,2560]{2,1,0:T(8,128)(2,1)S(1)} %copy-done.4), channel_id=1, replica_groups=mesh['section'=4,'ctx'=8] {'ctx'}, dimensions={1}, use_global_device_ids=true | all-gather | bytes 368640 | tf_op jit(solution)/shard_map/all_gather | solution.py:29
  106.2 7.9 %all_gather.18 = bf16[128,2560]{0,1:T(8,128)(2,1)S(1)} all-gather(bf16[128,640]{0,1:T(8,128)(2,1)S(1)} %copy.42), channel_id=1, replica_groups=mesh['section'=4,'ctx'=8] {'section'}, dimensions={1}, use_global_device_ids=true | all-gather | bytes 819200 | tf_op jit(solution)/shard_map/all_gather | solution.py:23
  114.1 8.0 %all_gather.16 = bf16[128,2560]{0,1:T(8,128)(2,1)S(1)} all-gather(bf16[128,640]{0,1:T(8,128)(2,1)S(1)} %copy.39), channel_id=1, replica_groups=mesh['section'=4,'ctx'=8] {'section'}, dimensions={1}, use_global_device_ids=true | all-gather | bytes 819200 | tf_op jit(solution)/shard_map/all_gather | solution.py:22
  122.4 61.5 %while.28 = (s32[]{:T(128)}, f32[20,64]{1,0:T(8,128)S(1)}, f32[20,64]{1,0:T(8,128)S(1)}, bf16[20,64,128]{2,1,0:T(8,128)(2,1)S(1)}, s32[20]{0:T(128)S(1)}, /*inde...) while((s32[]{:T(128)}, f32[20,64]{1,0:T(8,128)S(1)}, ...), condition=%wide.region_4.5_spmd.clone, body=%wide.region_1.4_spmd.clone.sunk | while | flops 2162565 | bytes 118451 | solution.py:66
  184.0 21.7 %pmax.7 = bf16[20,64]{1,0:T(8,128)(2,1)S(1)} all-reduce(bf16[20,64]{1,0:T(8,128)(2,1)S(1)} %convert_element_type.43), channel_id=1, replica_groups=mesh['section'=4,'ctx'=8] {'ctx'}, use_global_device_ids=true, to_apply=%region_5.6 | all-reduce | flops 1280 | bytes 5120 | tf_op jit(solution)/shard_map/pmax | solution.py:67
  205.7 33.0 %psum.7 = f32[20,64]{1,0:T(8,128)S(1)} all-reduce(f32[20,64]{1,0:T(8,128)S(1)} %fusion.44), channel_id=1, replica_groups=mesh['section'=4,'ctx'=8] {'ctx'}, use_global_device_ids=true, to_apply=%region_6.7 | all-reduce | flops 1280 | bytes 10240 | tf_op jit(solution)/shard_map/psum | solution.py:68
  238.7 92.9 %while.29 = (s32[]{:T(128)}, f32[20,64,128]{2,1,0:T(8,128)S(1)}, bf16[20,128,128]{1,2,0:T(8,128)(2,1)}, bf16[20,128,128]{1,2,0:T(8,128)(2,1)}, bf16[20,64,128]{2...) while((s32[]{:T(128)}, f32[20,64,128]{2,1,0:T(8,128)S(1)}, ...), condition=%wide.region_8.9_spmd.clone, body=%wide.region_7.8_spmd.clone.sunk | while | flops 10567685 | bytes 480487 | solution.py:86
  241.5 0.9 fusion.84
  242.5 0.8 fusion.83
  246.2 0.9 fusion.84
  247.2 0.8 fusion.83
  250.8 0.9 fusion.84
  255.4 0.9 fusion.84
  260.1 0.9 fusion.84
  264.7 0.9 fusion.84
  269.4 0.9 fusion.84
  274.0 0.9 fusion.84
  275.0 0.8 fusion.83
  278.7 0.9 fusion.84
  279.7 0.8 fusion.83
  283.3 0.9 fusion.84
  284.3 0.8 fusion.83
  287.9 0.9 fusion.84
  288.9 0.8 fusion.83
  292.6 0.9 fusion.84
  293.6 0.8 fusion.83
  297.2 0.9 fusion.84
  301.9 0.9 fusion.84
  302.9 0.8 fusion.83
  306.5 0.9 fusion.84
  307.5 0.8 fusion.83
  311.2 0.9 fusion.84
  312.2 0.8 fusion.83
  315.8 0.9 fusion.84
  320.5 0.9 fusion.84
  321.5 0.8 fusion.83
  325.1 0.9 fusion.84
  329.7 0.9 fusion.84
  330.8 0.8 fusion.83
  332.4 0.9 copy_bitcast_fusion
  333.3 17.2 %reduce-scatter.8.cloned.1.call-done = bf16[128,640]{0,1:T(8,128)(2,1)} async-done(((bf16[128,2560]{0,1:T(8,128)(2,1)}), bf16[128,640]{0,1:T(8,128)(2,1)}) %reduce-scatter.8.cloned.1.call-update) | async-done | bytes 163856 | tf_op jit(solution)/shard_map/reduce_scatter | solution.py:112
  350.5 1.7 copy.53
  352.2 23.3 %reduce-scatter.6.cloned.1.call-done = bf16[128,640]{0,1:T(8,128)(2,1)} async-done(((bf16[128,2560]{0,1:T(8,128)(2,1)}), bf16[128,640]{0,1:T(8,128)(2,1)}) %reduce-scatter.6.cloned.1.call-update) | async-done | bytes 163856 | tf_op jit(solution)/shard_map/reduce_scatter | solution.py:109
  375.5 1.7 copy.52
  377.2 64.4 %reduce-scatter.4.cloned.1.call-done = f32[1,8,2560]{2,1,0:T(8,128)} async-done(((f32[1,64,2560]{2,1,0:T(8,128)}), f32[1,8,2560]{2,1,0:T(8,128)}) %reduce-scatter.4.cloned.1.call-update) | async-done | bytes 81936 | tf_op jit(solution)/shard_map/reduce_scatter | solution.py:94
  441.6 1.5 convert_element_type.47
  (249 shorter events, 53.3 us)
Async XLA Ops:
  7.2 343.3 %reduce-scatter.8.cloned.1.call-start = ((), (), s32[]{:S(2)}) async-start(), calls=%async_computation.5 | async-start | bytes 819200 | tf_op jit(solution)/shard_map/reduce_scatter | solution.py:112
  7.3 0.7 copy-start.5
  9.2 33.0 %copy-start.2 = (bf16[1,8,2560]{2,1,0:T(8,128)(2,1)S(1)}, bf16[1,8,2560]{2,1,0:T(8,128)(2,1)}, u32[]{:S(2)}) copy-start(bf16[1,8,2560]{2,1,0:T(8,128)(2,1)} %param.15) | copy-start | bytes 122884
  9.2 33.0 %copy-start.3 = (bf16[1,8,2560]{2,1,0:T(8,128)(2,1)S(1)}, bf16[1,8,2560]{2,1,0:T(8,128)(2,1)}, u32[]{:S(2)}) copy-start(bf16[1,8,2560]{2,1,0:T(8,128)(2,1)} %param.14) | copy-start | bytes 122884
  42.2 30.9 %copy-start = (bf16[128,640]{1,0:T(8,128)(2,1)S(1)}, bf16[128,640]{1,0:T(8,128)(2,1)}, u32[]{:S(2)}) copy-start(bf16[128,640]{1,0:T(8,128)(2,1)} %param.12) | copy-start | bytes 491524
  73.1 0.9 copy-start.1
  74.0 0.8 copy-start.4
  331.6 43.9 %reduce-scatter.6.cloned.1.call-start = ((), (), s32[]{:S(2)}) async-start(), calls=%async_computation.4 | async-start | bytes 819200 | tf_op jit(solution)/shard_map/reduce_scatter | solution.py:109
  332.4 109.2 %reduce-scatter.4.cloned.1.call-start = ((), (), s32[]{:S(2)}) async-start(), calls=%async_computation.3 | async-start | bytes 737280 | tf_op jit(solution)/shard_map/reduce_scatter | solution.py:94
Sparse Core Ops, SparseCore 0:
  331.7 18.7 reduce-scatter.7
  353.0 22.4 reduce-scatter.5
  378.8 62.7 reduce-scatter.3
where the time goes:
time: 451 us; the launch traced here: 450 us
  blocking collectives  165 us (37%)
  waiting for transfers between devices  106 us (24%)
  loops' own time  78.6 us (17%)
  matrix products  46.9 us (10%)
  local copies, waits for them, and re-layouts  33.4 us (7%)
  between operations  14.6 us (3%)
  other arithmetic  5.47 us (1%)
    reduce_scatter x1, waiting for transfers between devices, local(): lax.psum_scatter(query_layout, 'ctx', scatter_dimension=1, tiled=True)  64.4 us
    another operation x1, loops' own time, local(): row_max, row_sum = lax.map(local_stats, (query_heads, head_ids))  39.3 us
    another operation x1, loops' own time, local(): lax.map(gradients, (query_heads, grad_heads, delta_heads, log_total, head...  39.3 us
    all_gather x1, blocking collectives, local(): lax.all_gather(grad_part, 'ctx', axis=1, tiled=True)  33 us
    psum x1, blocking collectives, local(): row_sum = lax.psum(row_sum * jnp.exp(row_max - peak_max), 'ctx')  33 us
    all_gather x1, blocking collectives, local(): lax.all_gather(query_part, 'ctx', axis=1, tiled=True)  30.8 us
    all_gather x1, blocking collectives, local(): delta_all = lax.all_gather(delta_part, 'ctx', axis=1, tiled=True)  30.6 us
    dynamic_slice x40, local copies, waits for them, and re-layouts, local(): row_max, row_sum = lax.map(local_stats, (query_heads, head_ids))  23.4 us
  transfers between devices with their start and end apart: 3, of which 3 were waited for; matrix products, arithmetic and copies ran while one was open for 1% of the time, Pallas kernels for 0%

commit v1 on v0

--- a/solution.py
+++ b/solution.py
@@ -6,6 +6,18 @@
 HEADS = 20
 HEAD_DIM = 128
 masked_score = -1e30
+
+
+def collect(x, axis, dim):
+    ways, here = (lax.axis_size(axis), lax.axis_index(axis))
+    grown, reach = (x, 1)
+    while reach < ways:
+        theirs = lax.ppermute(grown, axis, [(d, d ^ reach) for d in range(ways)])
+        mine_first = jnp.concatenate([grown, theirs], axis=dim)
+        theirs_first = jnp.concatenate([theirs, grown], axis=dim)
+        grown = jnp.where(here & reach == 0, mine_first, theirs_first)
+        reach = 2 * reach
+    return grown
 
 
 def local(block_order, queries, cache_keys, cache_values, attention_out, output_grad):
@@ -27,7 +39,7 @@
     pair_count = layers * group_heads
     query_all, grad_all = (
         lax.all_gather(query_part, "ctx", axis=1, tiled=True),
-        lax.all_gather(grad_part, "ctx", axis=1, tiled=True),
+        collect(grad_part, "ctx", 1),
     )
     delta_all = lax.all_gather(delta_part, "ctx", axis=1, tiled=True)
 

time: 451 us -> 433 us (0.960)
  blocking collectives: 165 us -> 131 us
  waiting for transfers between devices: 106 us -> 118 us
    all_gather x1 -> x0, blocking collectives: 33 us -> none  [local(): lax.all_gather(grad_part, 'ctx', axis=1, tiled=True)]
    ppermute x0 -> x3, waiting for transfers between devices: none -> 11.6 us  [collect(): theirs = lax.ppermute(grown, axis, [(d, d ^ reach) for d in range(ways)])]
  transfers between devices with their start and end apart: 3 -> 6, of which waited for: 3 -> 5; matrix products, arithmetic and copies ran while one was open for 1% -> 7% of each run, Pallas kernels for 0% -> 0%
where the time goes in v1:
time: 433 us; the launch traced here: 432 us
  blocking collectives  131 us (30%)
  waiting for transfers between devices  118 us (27%)
  loops' own time  78.6 us (18%)
  matrix products  46.9 us (11%)
  local copies, waits for them, and re-layouts  33.5 us (8%)
  between operations  14.6 us (3%)
  other arithmetic  5.7 us (1%)
    reduce_scatter x1, waiting for transfers between devices, local(): lax.psum_scatter(query_layout, 'ctx', scatter_dimension=1, tiled=True)  64.3 us
    another operation x1, loops' own time, local(): row_max, row_sum = lax.map(local_stats, (query_heads, head_ids))  39.3 us
    another operation x1, loops' own time, local(): lax.map(gradients, (query_heads, grad_heads, delta_heads, log_total, head...  39.3 us
    psum x1, blocking collectives, local(): row_sum = lax.psum(row_sum * jnp.exp(row_max - peak_max), 'ctx')  33 us
    all_gather x1, blocking collectives, local(): lax.all_gather(query_part, 'ctx', axis=1, tiled=True)  31.4 us
    all_gather x1, blocking collectives, local(): delta_all = lax.all_gather(delta_part, 'ctx', axis=1, tiled=True)  30.6 us
    dynamic_slice x40, local copies, waits for them, and re-layouts, local(): row_max, row_sum = lax.map(local_stats, (query_heads, head_ids))  23.4 us
    reduce_scatter x1, waiting for transfers between devices, local(): lax.psum_scatter(key_sum.astype(jnp.bfloat16), 'section', scatter_dimensi...  23.3 us
  transfers between devices with their start and end apart: 6, of which 5 were waited for; matrix products, arithmetic and copies ran while one was open for 7% of the time, Pallas kernels for 0%

profile of v1, /device:TPU:0, one launch (start us, length us, event | category | flops | bytes accessed | tf_op | source)
XLA Modules:
  0.0 431.8 jit_solution(29764947101411643)
XLA Ops:
  7.2 3.1 collective-permute-start
  12.2 1.1 copy.58
  14.1 31.4 %all_gather.12 = bf16[1,64,2560]{2,1,0:T(8,128)(2,1)S(1)} all-gather(bf16[1,8,2560]{2,1,0:T(8,128)(2,1)S(1)} %copy-done.3), channel_id=1, replica_groups=mesh['section'=4,'ctx'=8] {'ctx'}, dimensions={1}, use_global_device_ids=true | all-gather | bytes 368640 | tf_op jit(solution)/shard_map/all_gather | solution.py:41
  45.8 7.9 %all_gather.14 = bf16[128,2560]{0,1:T(8,128)(2,1)S(1)} all-gather(bf16[128,640]{0,1:T(8,128)(2,1)S(1)} %copy.65), channel_id=1, replica_groups=mesh['section'=4,'ctx'=8] {'section'}, dimensions={1}, use_global_device_ids=true | all-gather | bytes 819200 | tf_op jit(solution)/shard_map/all_gather | solution.py:35
  53.7 8.0 %all_gather.13 = bf16[128,2560]{0,1:T(8,128)(2,1)S(1)} all-gather(bf16[128,640]{0,1:T(8,128)(2,1)S(1)} %copy.58), channel_id=1, replica_groups=mesh['section'=4,'ctx'=8] {'section'}, dimensions={1}, use_global_device_ids=true | all-gather | bytes 819200 | tf_op jit(solution)/shard_map/all_gather | solution.py:34
  62.0 61.5 %while.28 = (s32[]{:T(128)}, f32[20,64]{1,0:T(8,128)S(1)}, f32[20,64]{1,0:T(8,128)S(1)}, bf16[20,64,128]{2,1,0:T(8,128)(2,1)S(1)}, s32[20]{0:T(128)S(1)}, /*inde...) while((s32[]{:T(128)}, f32[20,64]{1,0:T(8,128)S(1)}, ...), condition=%wide.region_4.5_spmd.clone, body=%wide.region_1.4_spmd.clone.sunk | while | flops 2162565 | bytes 118451 | solution.py:78
  123.5 20.6 %pmax.7 = bf16[20,64]{1,0:T(8,128)(2,1)S(1)} all-reduce(bf16[20,64]{1,0:T(8,128)(2,1)S(1)} %convert_element_type.43), channel_id=1, replica_groups=mesh['section'=4,'ctx'=8] {'ctx'}, use_global_device_ids=true, to_apply=%region_5.6 | all-reduce | flops 1280 | bytes 5120 | tf_op jit(solution)/shard_map/pmax | solution.py:79
  144.2 33.0 %psum.7 = f32[20,64]{1,0:T(8,128)S(1)} all-reduce(f32[20,64]{1,0:T(8,128)S(1)} %fusion.47), channel_id=1, replica_groups=mesh['section'=4,'ctx'=8] {'ctx'}, use_global_device_ids=true, to_apply=%region_6.7 | all-reduce | flops 1280 | bytes 10240 | tf_op jit(solution)/shard_map/psum | solution.py:80
  177.5 30.6 %all-gather = f32[64,20]{1,0:T(8,128)S(1)} all-gather(f32[8,20]{1,0:T(8,128)S(1)} %copy.66), channel_id=2, replica_groups=mesh['section'=4,'ctx'=8] {'ctx'}, dimensions={0}, use_global_device_ids=true | all-gather | bytes 5760 | tf_op jit(solution)/shard_map/all_gather | solution.py:44
  208.3 4.4 %collective-permute-done.1 = bf16[1,16,2560]{2,1,0:T(8,128)(2,1)S(1)} collective-permute-done((bf16[1,16,2560]{2,1,0:T(8,128)(2,1)S(1)}, bf16[1,16,2560]{2,1,0:T(8,128)(2,1)S(1)}, u32[]{:S(2)}, u32[]{:S(2)}) %collective-permute-start.1) | collective-permute-done | bytes 81952 | tf_op jit(solution)/shard_map/ppermute | solution.py:15
  213.0 7.2 %collective-permute-done.2 = bf16[1,32,2560]{2,1,0:T(8,128)(2,1)S(1)} collective-permute-done((bf16[1,32,2560]{2,1,0:T(8,128)(2,1)S(1)}, bf16[1,32,2560]{2,1,0:T(8,128)(2,1)S(1)}, u32[]{:S(2)}, u32[]{:S(2)}) %collective-permute-start.2) | collective-permute-done | bytes 163872 | tf_op jit(solution)/shard_map/ppermute | solution.py:15
  220.3 92.9 %while.29 = (s32[]{:T(128)}, f32[20,64,128]{2,1,0:T(8,128)S(1)}, bf16[20,128,128]{1,2,0:T(8,128)(2,1)}, bf16[20,128,128]{1,2,0:T(8,128)(2,1)}, bf16[20,64,128]{2...) while((s32[]{:T(128)}, f32[20,64,128]{2,1,0:T(8,128)S(1)}, ...), condition=%wide.region_8.9_spmd.clone, body=%wide.region_7.8_spmd.clone.sunk | while | flops 10567685 | bytes 480487 | solution.py:98
  223.2 0.9 fusion.88
  227.8 0.9 fusion.88
  228.8 0.8 fusion.87
  232.4 0.9 fusion.88
  237.1 0.9 fusion.88
  241.7 0.9 fusion.88
  246.4 0.9 fusion.88
  251.0 0.9 fusion.88
  255.6 0.9 fusion.88
  256.7 0.8 fusion.87
  260.3 0.9 fusion.88
  264.9 0.9 fusion.88
  269.6 0.9 fusion.88
  270.6 0.8 fusion.87
  274.2 0.9 fusion.88
  275.2 0.8 fusion.87
  278.9 0.9 fusion.88
  283.5 0.9 fusion.88
  284.5 0.8 fusion.87
  288.2 0.9 fusion.88
  289.2 0.8 fusion.87
  292.8 0.9 fusion.88
  293.8 0.8 fusion.87
  297.5 0.9 fusion.88
  302.1 0.9 fusion.88
  303.1 0.8 fusion.87
  306.7 0.9 fusion.88
  311.4 0.9 fusion.88
  312.4 0.8 fusion.87
  314.0 0.9 copy_bitcast_fusion
  314.9 17.8 %reduce-scatter.8.cloned.1.call-done = bf16[128,640]{0,1:T(8,128)(2,1)} async-done(((bf16[128,2560]{0,1:T(8,128)(2,1)}), bf16[128,640]{0,1:T(8,128)(2,1)}) %reduce-scatter.8.cloned.1.call-update) | async-done | bytes 163856 | tf_op jit(solution)/shard_map/reduce_scatter | solution.py:124
  332.7 1.7 copy.75
  334.4 23.3 %reduce-scatter.6.cloned.1.call-done = bf16[128,640]{0,1:T(8,128)(2,1)} async-done(((bf16[128,2560]{0,1:T(8,128)(2,1)}), bf16[128,640]{0,1:T(8,128)(2,1)}) %reduce-scatter.6.cloned.1.call-update) | async-done | bytes 163856 | tf_op jit(solution)/shard_map/reduce_scatter | solution.py:121
  357.7 1.7 copy.74
  359.4 64.3 %reduce-scatter.4.cloned.1.call-done = f32[1,8,2560]{2,1,0:T(8,128)} async-done(((f32[1,64,2560]{2,1,0:T(8,128)}), f32[1,8,2560]{2,1,0:T(8,128)}) %reduce-scatter.4.cloned.1.call-update) | async-done | bytes 81936 | tf_op jit(solution)/shard_map/reduce_scatter | solution.py:106
  423.8 1.5 convert_element_type.47
  (259 shorter events, 55.1 us)
Async XLA Ops:
  7.2 325.6 %reduce-scatter.8.cloned.1.call-start = ((), (), s32[]{:S(2)}) async-start(), calls=%async_computation.5 | async-start | bytes 819200 | tf_op jit(solution)/shard_map/reduce_scatter | solution.py:124
  7.2 200.9 %collective-permute-start = (bf16[1,8,2560]{2,1,0:T(8,128)(2,1)}, bf16[1,8,2560]{2,1,0:T(8,128)(2,1)S(1)}, u32[]{:S(2)}, u32[]{:S(2)}) collective-permute-start(bf16[1,8,2560]{2,1,0:T(8,128)(2,1)} %param.15), channel_id=1, source_target_pairs={{0,1},{1,0},{2,3},{3,2},{4,5},{5,4},{6,7},{7,6},{8,9},{9,8},{10,11... | collective-permute-start | bytes 122888 | tf_op jit(solution)/shard_map/ppermute | solution.py:15
  10.3 0.7 copy-start.4
  12.2 1.1 copy-start.1
  13.3 0.8 copy-start.3
  144.2 33.0 %copy-start = (bf16[1,8,2560]{2,1,0:T(8,128)(2,1)S(1)}, bf16[1,8,2560]{2,1,0:T(8,128)(2,1)}, u32[]{:S(2)}) copy-start(bf16[1,8,2560]{2,1,0:T(8,128)(2,1)} %param.15) | copy-start | bytes 122884
  144.2 33.0 %copy-start.2 = (bf16[1,8,2560]{2,1,0:T(8,128)(2,1)S(1)}, bf16[1,8,2560]{2,1,0:T(8,128)(2,1)}, u32[]{:S(2)}) copy-start(bf16[1,8,2560]{2,1,0:T(8,128)(2,1)} %param.14) | copy-start | bytes 122884
  208.2 4.5 %collective-permute-start.1 = (bf16[1,16,2560]{2,1,0:T(8,128)(2,1)S(1)}, bf16[1,16,2560]{2,1,0:T(8,128)(2,1)S(1)}, u32[]{:S(2)}, u32[]{:S(2)}) collective-permute-start(bf16[1,16,2560]{2,1,0:T(8,128)(2,1)S(1)} %maximum_select_fusion.4), channel_id=1, source_target_pairs={{0,2},{1,3},{2,0},{3,1},{4,6},{5,7},{6,4},{7,5},{8,10},{9,11},{10,... | collective-permute-start | bytes 245768 | tf_op jit(solution)/shard_map/ppermute | solution.py:15
  212.7 7.5 %collective-permute-start.2 = (bf16[1,32,2560]{2,1,0:T(8,128)(2,1)S(1)}, bf16[1,32,2560]{2,1,0:T(8,128)(2,1)S(1)}, u32[]{:S(2)}, u32[]{:S(2)}) collective-permute-start(bf16[1,32,2560]{2,1,0:T(8,128)(2,1)S(1)} %maximum_select_fusion.2), channel_id=1, source_target_pairs={{0,4},{1,5},{2,6},{3,7},{4,0},{5,1},{6,2},{7,3},{8,12},{9,13},{10,... | collective-permute-start | bytes 491528 | tf_op jit(solution)/shard_map/ppermute | solution.py:15
  313.2 44.5 %reduce-scatter.6.cloned.1.call-start = ((), (), s32[]{:S(2)}) async-start(), calls=%async_computation.4 | async-start | bytes 819200 | tf_op jit(solution)/shard_map/reduce_scatter | solution.py:121
  314.0 109.8 %reduce-scatter.4.cloned.1.call-start = ((), (), s32[]{:S(2)}) async-start(), calls=%async_computation.3 | async-start | bytes 737280 | tf_op jit(solution)/shard_map/reduce_scatter | solution.py:106
Sparse Core Ops, SparseCore 0:
  313.4 19.3 reduce-scatter.7
  335.2 22.4 reduce-scatter.5
  361.0 62.7 reduce-scatter.3
